TPU v7x, 256 devices: a whole 4x4x8 slice. The times are simulated.
256 devices in a mesh: seq: 32 (over y, z), tensor: 8 (over x, core).
Axes of the slice: x: 4, y: 4, z: 8, core: 2. Of those that a mesh axis runs over, the one named last changes fastest.
Arguments:
- state: bfloat16 [32768, 2048], P('seq', 'tensor'), may hold values from -20.5 to 20.5
- memory: bfloat16 [512, 2048], P('seq', 'tensor'), may hold values from -20.5 to 20.5
- w_query: bfloat16 [2048, 2048], P('seq', 'tensor'), may hold values from -0.1875 to 0.1875
- w_key: bfloat16 [2048, 2048], P('seq', 'tensor'), may hold values from -0.1875 to 0.1875
- w_value: bfloat16 [2048, 2048], P('seq', 'tensor'), may hold values from -0.125 to 0.125
- w_output: bfloat16 [2048, 2048], P('tensor', 'seq'), may hold values from -0.375 to 0.375
- norm_gain: float32 [2048], P('tensor'), may hold values from 0.1 to 1.9
- remaining: int32 [32768], P('seq'), may hold values from 0 to 3
- slot_home: int32 [512], replicated, may hold values from 0 to 31
Outputs:
- new_state: bfloat16 [32768, 2048], P('seq', 'tensor')
- new_memory: bfloat16 [512, 2048], P('seq', 'tensor')
Inputs may be any that keep to these rules, and one draw needn't show every extreme that they name: `remaining`: 0 means the token has halted.
All inputs are finite; a program needn't handle non-finite values.
Results may differ from a plain program's by a relative error of at most 0.014.
The roundings to bfloat16 on the way count: a program that leaves them out, or rounds other values in their place, can miss the bound.
Values may be sent and summed in bfloat16 or wider, within the bound.
No kernel may reach another device: no remote copies, remote signals or barrier semaphores. Data moves between devices by JAX's collectives and lax.ppermute only.
A program may use at most 128 MiB of HBM per device.

v0:
```python
import math
import jax
import jax.numpy as jnp
from jax import lax
from jax.sharding import PartitionSpec as P

D = 2048
H = 16
HD = 128
HALF = 256
QB = 512
EPS = 1e-05
MASKED = -1e30


def with_halo(array, sides, width):
    for axis, dim in sides:
        peers, length = (lax.axis_size(axis), array.shape[dim])
        up = [(i, (i + 1) % peers) for i in range(peers - 1)]
        down = [(j, i) for i, j in up]
        last = lax.slice_in_dim(array, length - width, length, axis=dim)
        initial = lax.slice_in_dim(array, 0, width, axis=dim)
        before = lax.ppermute(last, axis, up)
        after = lax.ppermute(initial, axis, down)
        array = jnp.concatenate([before, array, after], axis=dim)
    return array


def merged(part, axis, combine):
    gathered = jax.tree.map(lambda a: lax.all_gather(a, axis), part)

    def take(source):
        return jax.tree.map(lambda a: lax.dynamic_index_in_dim(a, source, 0, False), gathered)

    return lax.fori_loop(
        1, lax.axis_size(axis), lambda source, state: combine(state, take(source)), take(0)
    )


def head_slopes(first, amount):
    order = (first + jnp.arange(amount, dtype=jnp.int32)).astype(jnp.float32)
    return 0.25 * 8.0 ** (order / (H - 1))


def shards(state, memory, w_query, w_key, w_value, w_output, norm_gain, remaining, slot_home):
    tok_rows = state.shape[0]
    slot_rows = memory.shape[0]
    seq_count = lax.axis_size("seq")
    seq_place = lax.axis_index("seq")
    tensor_place = lax.axis_index("tensor")
    local_width = w_query.shape[1]
    local_heads = local_width // HD
    total_tokens = tok_rows * seq_count
    score_scale = 1.0 / math.sqrt(HD)
    distance_slopes = head_slopes(tensor_place * local_heads, local_heads)
    homes = slot_home.astype(jnp.float32)
    home_gap = jnp.abs(homes - seq_place.astype(jnp.float32))
    slot_bias = distance_slopes[:, None] * home_gap[None, :]
    state_full, memory_full = (
        lax.all_gather(state, "tensor", axis=1, tiled=True),
        lax.all_gather(memory, "tensor", axis=1, tiled=True),
    )
    rows_full = jnp.concatenate([state_full, memory_full], axis=0)
    pieces = (
        lax.all_gather(w_query, "seq", axis=0, tiled=True),
        lax.all_gather(w_key, "seq", axis=0, tiled=True),
        lax.all_gather(w_value, "seq", axis=0, tiled=True),
    )
    query_acc, key_acc, value_acc = tuple(
        (jnp.dot(rows_full, piece, preferred_element_type=jnp.float32) for piece in pieces)
    )
    query = query_acc.astype(jnp.bfloat16)
    keys = key_acc.astype(jnp.bfloat16)
    values = value_acc.astype(jnp.bfloat16)
    slot_heads = jnp.concatenate([query[tok_rows:], keys[tok_rows:], values[tok_rows:]], axis=1)
    all_slots = lax.all_gather(slot_heads, "seq", axis=0, tiled=True)
    memory_slot_query = all_slots[:, :local_width].reshape(-1, local_heads, HD)
    memory_slot_keys = all_slots[:, local_width : 2 * local_width].reshape(-1, local_heads, HD)
    memory_slot_values = all_slots[:, 2 * local_width :].reshape(-1, local_heads, HD)
    token_key_rows = keys[:tok_rows].reshape(tok_rows, local_heads, HD)
    token_value_rows = values[:tok_rows].reshape(tok_rows, local_heads, HD)
    keys_values = jnp.concatenate([keys[:tok_rows], values[:tok_rows]], axis=1)
    padded = with_halo(keys_values, (("seq", 0),), HALF)
    block = QB
    window_extent = block + 2 * HALF

    def one_block(number):
        start = number * block
        query_matrix = lax.dynamic_slice_in_dim(query, start, block, 0).reshape(
            block, local_heads, HD
        )
        near_rows = lax.dynamic_slice_in_dim(padded, start, window_extent, 0)
        near_keys = near_rows[:, :local_width].reshape(window_extent, local_heads, HD)
        near_values = near_rows[:, local_width:].reshape(window_extent, local_heads, HD)
        near = (
            jnp.einsum("qhd,khd->hqk", query_matrix, near_keys, preferred_element_type=jnp.float32)
            * score_scale
        )
        first = seq_place * tok_rows + start
        qpos = first + jnp.arange(block, dtype=jnp.int32)
        kpos = first - HALF + jnp.arange(window_extent, dtype=jnp.int32)
        valid = (
            (jnp.abs(qpos[:, None] - kpos[None, :]) <= HALF)
            & (kpos >= 0)[None, :]
            & (kpos < total_tokens)[None, :]
        )
        near = jnp.where(valid[None], near, MASKED)
        distant_mask = (
            jnp.einsum(
                "taw,caw->atc", query_matrix, memory_slot_keys, preferred_element_type=jnp.float32
            )
            * score_scale
            - slot_bias[:, None, :]
        )
        scores = jnp.concatenate([near, distant_mask], axis=2)
        top = jnp.max(scores, axis=2, keepdims=True)
        exponent_terms = jnp.exp(scores - top)
        total = jnp.sum(exponent_terms, axis=2)
        attention_probabilities = exponent_terms.astype(jnp.bfloat16)
        numer = jnp.einsum(
            "hqk,khd->qhd",
            attention_probabilities[:, :, :window_extent],
            near_values,
            preferred_element_type=jnp.float32,
        )
        numer = numer + jnp.einsum(
            "lse,elf->slf",
            attention_probabilities[:, :, window_extent:],
            memory_slot_values,
            preferred_element_type=jnp.float32,
        )
        return (
            (numer / jnp.transpose(total)[:, :, None])
            .astype(jnp.bfloat16)
            .reshape(block, local_width)
        )

    token_mix = lax.map(one_block, jnp.arange(tok_rows // block, dtype=jnp.int32)).reshape(
        tok_rows, local_width
    )
    unnormalized_scores = (
        jnp.einsum(
            "gki,pki->kgp", memory_slot_query, token_key_rows, preferred_element_type=jnp.float32
        )
        * score_scale
        - slot_bias[:, :, None]
    )
    local_top = jnp.max(unnormalized_scores, axis=2)
    exponent_terms = jnp.exp(unnormalized_scores - local_top[:, :, None])
    local_sum = jnp.transpose(jnp.sum(exponent_terms, axis=2))
    local_num = jnp.einsum(
        "xzg,gxw->zxw",
        exponent_terms.astype(jnp.bfloat16),
        token_value_rows,
        preferred_element_type=jnp.float32,
    )
    local_top = jnp.transpose(local_top)

    def combine(first_part, second_part):
        top = jnp.maximum(first_part[0], second_part[0])
        weight_first = jnp.exp(first_part[0] - top)
        weight_second = jnp.exp(second_part[0] - top)
        sums = weight_first * first_part[1] + weight_second * second_part[1]
        numers = (
            weight_first[:, :, None] * first_part[2] + weight_second[:, :, None] * second_part[2]
        )
        return (top, sums, numers)

    merged_parts = merged((local_top, local_sum, local_num), "seq", combine)
    own_sum = lax.dynamic_slice_in_dim(merged_parts[1], seq_place * slot_rows, slot_rows, 0)
    own_num = lax.dynamic_slice_in_dim(merged_parts[2], seq_place * slot_rows, slot_rows, 0)
    slot_mix = (own_num / own_sum[:, :, None]).astype(jnp.bfloat16).reshape(slot_rows, local_width)
    mixed = jnp.concatenate([token_mix, slot_mix], axis=0)
    partial_rows = jnp.dot(
        mixed,
        lax.all_gather(w_output, "seq", axis=1, tiled=True),
        preferred_element_type=jnp.float32,
    )
    summed = lax.psum_scatter(
        partial_rows.astype(jnp.bfloat16), "tensor", scatter_dimension=1, tiled=True
    ).astype(jnp.float32)
    residual = jnp.concatenate([state, memory], axis=0).astype(jnp.float32) + summed
    squares = lax.psum(jnp.sum(residual * residual, axis=1), "tensor")
    normed_rows = (residual * lax.rsqrt(squares / D + EPS)[:, None] * norm_gain[None, :]).astype(
        jnp.bfloat16
    )
    new_state = jnp.where((remaining > 0)[:, None], normed_rows[:tok_rows], state)
    new_memory = normed_rows[tok_rows:]
    return (new_state, new_memory)


def solution(mesh):
    placed = (
        P("seq", "tensor"),
        P("seq", "tensor"),
        P("seq", "tensor"),
        P("seq", "tensor"),
        P("seq", "tensor"),
        P("tensor", "seq"),
        P("tensor"),
        P("seq"),
        P(),
    )
    return jax.shard_map(
        shards,
        mesh=mesh,
        in_specs=placed,
        out_specs=(P("seq", "tensor"), P("seq", "tensor")),
        check_vma=False,
    )
```

profile of v0, /device:TPU:1, one launch (start us, length us, event | category | flops | bytes accessed | tf_op | source)
XLA Modules:
  0.0 714.2 jit_solution(8940133622111685820)
XLA Ops:
  10.7 16.0 %all_gather.40 = bf16[16,2048]{1,0:T(8,128)(2,1)S(1)} all-gather(bf16[16,256]{1,0:T(8,128)(2,1)} %param.14), channel_id=1, replica_groups=mesh['seq'=32,'tensor'=8] {'tensor'}, dimensions={1}, use_global_device_ids=true | all-gather | bytes 73728 | tf_op jit(solution)/shard_map/all_gather | solution.py:61
  26.8 25.3 %all-gather.10.cloned.1.call-done = bf16[1024,2048]{1,0:T(8,128)(2,1)} async-done(((bf16[1024,256]{1,0:T(8,128)(2,1)}), bf16[1024,2048]{1,0:T(8,128)(2,1)}) %all-gather.10.cloned.1.call-update) | async-done | bytes 4194320 | tf_op jit(solution)/shard_map/all_gather | solution.py:60
  52.1 4.7 constant_dynamic-update-slice_fusion.2
  57.4 69.1 %all-gather.14.cloned.1.call-done = bf16[2048,256]{1,0:T(8,128)(2,1)} async-done(((bf16[64,256]{1,0:T(8,128)(2,1)}), bf16[2048,256]{1,0:T(8,128)(2,1)}) %all-gather.14.cloned.1.call-update) | async-done | bytes 1048592 | tf_op jit(solution)/shard_map/all_gather | solution.py:67
  126.5 3.8 convolution_convert_fusion.2
  130.4 72.6 %all-gather.12.cloned.1.call-done = bf16[2048,256]{1,0:T(8,128)(2,1)} async-done(((bf16[64,256]{1,0:T(8,128)(2,1)}), bf16[2048,256]{1,0:T(8,128)(2,1)}) %all-gather.12.cloned.1.call-update) | async-done | bytes 1048592 | tf_op jit(solution)/shard_map/all_gather | solution.py:66
  203.0 3.8 convolution_convert_fusion.3
  206.9 72.4 %all-gather.16.cloned.1.call-done = bf16[2048,256]{1,0:T(8,128)(2,1)} async-done(((bf16[64,256]{1,0:T(8,128)(2,1)}), bf16[2048,256]{1,0:T(8,128)(2,1)}) %all-gather.16.cloned.1.call-update) | async-done | bytes 1048592 | tf_op jit(solution)/shard_map/all_gather | solution.py:65
  279.3 3.8 convolution_convert_fusion.1
  284.1 36.9 %all_gather.44 = bf16[512,768]{1,0:T(8,128)(2,1)S(1)} all-gather(bf16[16,768]{1,0:T(8,128)(2,1)S(1)} %pad_maximum_fusion.4), channel_id=1, replica_groups=mesh['seq'=32,'tensor'=8] {'seq'}, dimensions={0}, use_global_device_ids=true | all-gather | bytes 811008 | tf_op jit(solution)/shard_map/all_gather | solution.py:76
  332.0 36.6 %all-gather = f32[16384,2]{0,1:T(2,128)S(1)} all-gather(f32[512,2]{0,1:T(2,128)S(1)} %bitcast.123), channel_id=2, replica_groups=mesh['seq'=32,'tensor'=8] {'seq'}, dimensions={0}, use_global_device_ids=true | all-gather | bytes 135168 | tf_op jit(solution)/shard_map/all_gather | solution.py:30
  371.9 35.7 %all-gather.1 = f32[16384,2]{0,1:T(2,128)S(1)} all-gather(f32[512,2]{0,1:T(2,128)S(1)} %bitcast.126), channel_id=3, replica_groups=mesh['seq'=32,'tensor'=8] {'seq'}, dimensions={0}, use_global_device_ids=true | all-gather | bytes 135168 | tf_op jit(solution)/shard_map/all_gather | solution.py:30
  409.9 22.6 %while.33 = (s32[]{:T(128)}, bf16[2,512,256]{2,1,0:T(8,128)(2,1)}, s32[2]{0:T(128)}, bf16[1536,512]{1,0:T(8,128)(2,1)S(1)}, s32[]{:T(128)}, /*index=5*/bf16[1040...) while((s32[]{:T(128)}, bf16[2,512,256]{2,1,0:T(8,128)(2,1)}, ...), condition=%wide.region_4.5_spmd.clone, body=%wide.region_0.4_spmd.clone.sunk | while | flops 819334656 | bytes 41282024 | solution.py:138
  432.4 48.4 %all-gather.20.cloned.1.call-done = f32[16384,2,128]{0,2,1:T(8,128)} async-done(((f32[512,2,128]{0,2,1:T(8,128)}), f32[16384,2,128]{0,2,1:T(8,128)}) %all-gather.20.cloned.1.call-update) | async-done | bytes 16777232 | tf_op jit(solution)/shard_map/all_gather | solution.py:30
  482.2 25.0 %copy.46 = f32[16384,2,128]{2,1,0:T(2,128)} copy(f32[16384,2,128]{0,2,1:T(8,128)} %all-gather.20.cloned.1.call-done) | data formatting | bytes 33554432 | tf_op jit(solution)/shard_map/while | solution.py:35
  507.1 140.4 %while.32 = (s32[]{:T(128)}, f32[512,2]{0,1:T(2,128)S(1)}, f32[512,2]{0,1:T(2,128)S(1)}, f32[512,2,128]{2,1,0:T(2,128)S(1)}, f32[32,512,2]{1,2,0:T(2,128)S(1)}, ...) while((s32[]{:T(128)}, f32[512,2]{0,1:T(2,128)S(1)}, ...), condition=%wide.region_8.9_spmd, body=%wide.region_7.8_spmd.sunk | while | flops 399365 | bytes 1630351 | solution.py:35
  508.2 3.5 fusion.77
  512.7 3.5 fusion.77
  517.3 3.5 fusion.77
  539.9 3.5 fusion.77
  544.5 3.5 fusion.77
  647.9 4.5 convolution_convert_fusion
  653.1 34.7 %reduce-scatter.2.cloned.1.call-done = bf16[1040,256]{1,0:T(8,128)(2,1)} async-done(((bf16[1040,2048]{1,0:T(8,128)(2,1)}), bf16[1040,256]{1,0:T(8,128)(2,1)}) %reduce-scatter.2.cloned.1.call-update) | async-done | bytes 532496 | tf_op jit(solution)/shard_map/reduce_scatter | solution.py:179
  689.1 15.3 %psum.7 = f32[1040]{0:T(1024)S(1)} all-reduce(f32[1040]{0:T(1024)S(1)} %multiply_reduce_fusion), channel_id=1, replica_groups=mesh['seq'=32,'tensor'=8] {'tensor'}, use_global_device_ids=true, to_apply=%region_11.12 | all-reduce | flops 1040 | bytes 8320 | tf_op jit(solution)/shard_map/psum | solution.py:183
  (257 shorter events, 170.8 us)
Async XLA Ops:
  7.2 44.9 %all-gather.10.cloned.1.call-start = ((), (), s32[]{:S(2)}) async-start(), calls=%async_computation.1 | async-start | bytes 4718592 | tf_op jit(solution)/shard_map/all_gather | solution.py:60
  7.9 118.6 %all-gather.14.cloned.1.call-start = ((), (), s32[]{:S(2)}) async-start(), calls=%async_computation.3 | async-start | bytes 1081344 | tf_op jit(solution)/shard_map/all_gather | solution.py:67
  8.6 194.4 %all-gather.12.cloned.1.call-start = ((), (), s32[]{:S(2)}) async-start(), calls=%async_computation.2 | async-start | bytes 1081344 | tf_op jit(solution)/shard_map/all_gather | solution.py:66
  9.4 270.0 %all-gather.16.cloned.1.call-start = ((), (), s32[]{:S(2)}) async-start(), calls=%async_computation.4 | async-start | bytes 1081344 | tf_op jit(solution)/shard_map/all_gather | solution.py:65
  10.0 470.9 %all-gather.20.cloned.1.call-start = ((), (), s32[]{:S(2)}) async-start(), calls=%async_computation.7 | async-start | bytes 17301504 | tf_op jit(solution)/shard_map/all_gather | solution.py:30
  10.7 46.1 %copy-start.11 = (f32[512]{0:T(512)}, f32[512]{0:T(512)S(1)}, u32[]{:S(2)}) copy-start(f32[512]{0:T(512)S(1)} %subtract_abs_fusion) | copy-start | bytes 6148
  26.7 30.1 %copy-start.14 = (f32[2]{0:T(128)}, f32[2]{0:T(128)S(1)}, u32[]{:S(2)}) copy-start(f32[2]{0:T(128)S(1)} %power_multiply_fusion) | copy-start | bytes 28
  26.8 295.1 %copy-start.13 = (f32[2,512]{1,0:T(2,128)}, f32[2,512]{1,0:T(2,128)S(1)}, u32[]{:S(2)}) copy-start(f32[2,512]{1,0:T(2,128)S(1)} %broadcast_multiply_fusion.1) | copy-start | bytes 12292
  284.1 39.7 %copy-start.8 = (bf16[1024,256]{0,1:T(8,128)(2,1)S(1)}, bf16[1024,256]{0,1:T(8,128)(2,1)}, u32[]{:S(2)}) copy-start(bf16[1024,256]{0,1:T(8,128)(2,1)} %copy.45) | copy-start | bytes 1572868
  321.9 1.9 copy-start
  325.9 322.0 %all-gather.18.cloned.1.call-start = ((), (), s32[]{:S(2)}) async-start(), calls=%async_computation.5 | async-start | bytes 1081344 | tf_op jit(solution)/shard_map/all_gather | solution.py:176
  326.5 361.3 %reduce-scatter.2.cloned.1.call-start = ((), (), s32[]{:S(2)}) async-start(), calls=%async_computation.6 | async-start | bytes 4792320 | tf_op jit(solution)/shard_map/reduce_scatter | solution.py:179
  326.6 81.1 %collective-permute-start = (bf16[256,512]{1,0:T(8,128)(2,1)S(1)}, bf16[256,512]{1,0:T(8,128)(2,1)S(1)}, u32[]{:S(2)}, u32[]{:S(2)}) collective-permute-start(bf16[256,512]{1,0:T(8,128)(2,1)S(1)} %get-tuple-element.403), channel_id=1, source_target_pairs={{0,8},{8,16},{16,24},{24,32},{32,40},{40,48},{48,56},{56,64},{64,7... | collective-permute-start | bytes 786440 | tf_op jit(solution)/shard_map/ppermute | solution.py:23
  329.1 79.2 %collective-permute-start.1 = (bf16[256,512]{1,0:T(8,128)(2,1)S(1)}, bf16[256,512]{1,0:T(8,128)(2,1)}, u32[]{:S(2)}, u32[]{:S(2)}) collective-permute-start(bf16[256,512]{1,0:T(8,128)(2,1)S(1)} %get-tuple-element.404), channel_id=1, source_target_pairs={{8,0},{16,8},{24,16},{32,24},{40,32},{48,40},{56,48},{64,56},{72,6... | collective-permute-start | bytes 786440 | tf_op jit(solution)/shard_map/ppermute | solution.py:24
  409.9 2.9 copy-start.3
  417.6 2.1 copy-start.9
  418.8 2.3 copy-start.4
  421.1 2.9 copy-start.3
  428.8 2.1 copy-start.9
  430.1 2.3 copy-start.4
  507.1 140.7 %copy-start.7 = (bf16[2,512,256]{2,1,0:T(8,128)(2,1)S(1)}, bf16[2,512,256]{2,1,0:T(8,128)(2,1)}, u32[]{:S(2)}) copy-start(bf16[2,512,256]{2,1,0:T(8,128)(2,1)} %get-tuple-element.294) | copy-start | bytes 1572868
  652.4 35.4 %copy-start.2 = (bf16[1024,256]{1,0:T(8,128)(2,1)S(1)}, bf16[1024,256]{1,0:T(8,128)(2,1)}, u32[]{:S(2)}) copy-start(bf16[1024,256]{1,0:T(8,128)(2,1)} %param.13) | copy-start | bytes 1572868
  652.4 35.4 %copy-start.12 = (bf16[16,256]{1,0:T(8,128)(2,1)S(1)}, bf16[16,256]{1,0:T(8,128)(2,1)}, u32[]{:S(2)}) copy-start(bf16[16,256]{1,0:T(8,128)(2,1)} %param.14) | copy-start | bytes 24580
  652.4 52.0 %copy-start.16 = (f32[256]{0:T(256)S(1)}, f32[256]{0:T(256)}, u32[]{:S(2)}) copy-start(f32[256]{0:T(256)} %param.19) | copy-start | bytes 3076
  (8 other events, 8.5 us)
Sparse Core Ops, SparseCore 0:
  9.8 42.2 all-gather.9
  54.7 71.8 all-gather.13
  129.1 73.8 all-gather.11
  205.5 73.8 all-gather.15
  326.0 154.7 all-gather.19
  483.3 68.5 all-gather.17
  652.5 35.1 reduce-scatter.1
where the time goes:
time: 718 us; the launch traced here: 714 us
  waiting for transfers between devices  326 us (45%)
  other arithmetic  144 us (20%)
  blocking collectives  141 us (20%)
  local copies, waits for them, and re-layouts  55.6 us (8%)
  matrix products  26.7 us (4%)
  between operations  14.4 us (2%)
    add x31, other arithmetic, combine(): weight_first[:, :, None] * first_part[2]  108 us
    all_gather x1, waiting for transfers between devices, shards(): lax.all_gather(w_key, 'seq', axis=0, tiled=True)  72.6 us
    all_gather x1, waiting for transfers between devices, shards(): lax.all_gather(w_query, 'seq', axis=0, tiled=True)  72.4 us
    all_gather x2, blocking collectives, merged(): gathered = jax.tree.map(lambda a: lax.all_gather(a, axis), part)  72.3 us
    all_gather x1, waiting for transfers between devices, shards(): lax.all_gather(w_value, 'seq', axis=0, tiled=True)  69.1 us
    all_gather x1, waiting for transfers between devices, merged(): gathered = jax.tree.map(lambda a: lax.all_gather(a, axis), part)  48.4 us
    all_gather x1, blocking collectives, shards(): all_slots = lax.all_gather(slot_heads, 'seq', axis=0, tiled=True)  36.9 us
    reduce_scatter x1, waiting for transfers between devices, shards(): lax.psum_scatter(partial_rows.astype(jnp.bfloat16), 'tensor', scatter_dim...  34.7 us
  transfers between devices with their start and end apart: 9, of which 6 were waited for; matrix products, arithmetic and copies ran while one was open for 29% of the time, Pallas kernels for 0%

commit v1 on v0

--- a/solution.py
+++ b/solution.py
@@ -11,6 +11,13 @@
 QB = 512
 EPS = 1e-05
 MASKED = -1e30
+
+
+def gather_over(array, mesh_axis, dim):
+    peers = lax.axis_size(mesh_axis)
+    shards = jnp.stack([array for _ in range(peers)])
+    shards = lax.all_to_all(shards, mesh_axis, split_axis=0, concat_axis=0)
+    return jnp.concatenate(shards, axis=dim)
 
 
 def with_halo(array, sides, width):
@@ -63,7 +70,7 @@
     rows_full = jnp.concatenate([state_full, memory_full], axis=0)
     pieces = (
         lax.all_gather(w_query, "seq", axis=0, tiled=True),
-        lax.all_gather(w_key, "seq", axis=0, tiled=True),
+        gather_over(w_key, "seq", 0),
         lax.all_gather(w_value, "seq", axis=0, tiled=True),
     )
     query_acc, key_acc, value_acc = tuple(

time: 718 us -> 642 us (0.89)
  waiting for transfers between devices: 326 us -> 238 us
  starting transfers between devices: 4.04 us -> 16 us
    all_gather x1 -> x0, waiting for transfers between devices: 72.6 us -> none  [shards(): lax.all_gather(w_key, 'seq', axis=0, tiled=True)]
    all_to_all x0 -> x1, starting transfers between devices: none -> 12 us  [gather_over(): shards = lax.all_to_all(shards, mesh_axis, split_axis=0, concat_axis=0)]
    all_gather x1, waiting for transfers between devices: 25.3 us -> 13.9 us  [shards(): lax.all_gather(state, 'tensor', axis=1, tiled=True)]
  transfers between devices with their start and end apart: 9 -> 9, of which waited for: 6 -> 5; matrix products, arithmetic and copies ran while one was open for 29% -> 32% of each run, Pallas kernels for 0% -> 0%
where the time goes in v1:
time: 642 us; the launch traced here: 638 us
  waiting for transfers between devices  238 us (37%)
  other arithmetic  144 us (22%)
  blocking collectives  139 us (22%)
  local copies, waits for them, and re-layouts  57.6 us (9%)
  matrix products  26.4 us (4%)
  starting transfers between devices  16 us (2%)
  between operations  14.4 us (2%)
    add x31, other arithmetic, combine(): weight_first[:, :, None] * first_part[2]  108 us
    all_gather x2, blocking collectives, merged(): gathered = jax.tree.map(lambda a: lax.all_gather(a, axis), part)  72.4 us
    all_gather x1, waiting for transfers between devices, shards(): lax.all_gather(w_value, 'seq', axis=0, tiled=True)  69.1 us
    all_gather x1, waiting for transfers between devices, shards(): lax.all_gather(w_query, 'seq', axis=0, tiled=True)  69 us
    all_gather x1, waiting for transfers between devices, merged(): gathered = jax.tree.map(lambda a: lax.all_gather(a, axis), part)  48.2 us
    all_gather x1, blocking collectives, shards(): all_slots = lax.all_gather(slot_heads, 'seq', axis=0, tiled=True)  36.9 us
    reduce_scatter x1, waiting for transfers between devices, shards(): lax.psum_scatter(partial_rows.astype(jnp.bfloat16), 'tensor', scatter_dim...  34.6 us
    while x2, local copies, waits for them, and re-layouts, merged(): lax.fori_loop(1, lax.axis_size(axis), lambda source, state: combine(state...  25.2 us
  transfers between devices with their start and end apart: 9, of which 5 were waited for; matrix products, arithmetic and copies ran while one was open for 32% of the time, Pallas kernels for 0%

profile of v1, /device:TPU:1, one launch (start us, length us, event | category | flops | bytes accessed | tf_op | source)
XLA Modules:
  0.0 637.9 jit_solution(4023884986396734685)
XLA Ops:
  10.5 12.0 %all-to-all-start = ((bf16[32,64,256]{2,1,0:T(8,128)(2,1)}), bf16[32,64,256]{2,1,0:T(8,128)(2,1)S(1)}, u32[]{:S(2)}, u32[]{:S(2)}) async-start(bf16[32,64,256]{2,1,0:T(8,128)(2,1)} %stack.2), calls=%async_computation | async-start | bytes 2097152 | tf_op jit(solution)/shard_map/all_to_all | solution.py:19
  24.0 14.2 %all_gather.37 = bf16[16,2048]{1,0:T(8,128)(2,1)S(1)} all-gather(bf16[16,256]{1,0:T(8,128)(2,1)} %param.14), channel_id=1, replica_groups=mesh['seq'=32,'tensor'=8] {'tensor'}, dimensions={1}, use_global_device_ids=true | all-gather | bytes 73728 | tf_op jit(solution)/shard_map/all_gather | solution.py:68
  38.3 13.9 %all-gather.9.cloned.1.call-done = bf16[1024,2048]{1,0:T(8,128)(2,1)} async-done(((bf16[1024,256]{1,0:T(8,128)(2,1)}), bf16[1024,2048]{1,0:T(8,128)(2,1)}) %all-gather.9.cloned.1.call-update) | async-done | bytes 4194320 | tf_op jit(solution)/shard_map/all_gather | solution.py:67
  52.3 4.7 constant_dynamic-update-slice_fusion.2
  57.6 69.1 %all-gather.11.cloned.1.call-done = bf16[2048,256]{1,0:T(8,128)(2,1)} async-done(((bf16[64,256]{1,0:T(8,128)(2,1)}), bf16[2048,256]{1,0:T(8,128)(2,1)}) %all-gather.11.cloned.1.call-update) | async-done | bytes 1048592 | tf_op jit(solution)/shard_map/all_gather | solution.py:74
  126.7 3.8 convolution_convert_fusion.2
  134.2 69.0 %all-gather.13.cloned.1.call-done = bf16[2048,256]{1,0:T(8,128)(2,1)} async-done(((bf16[64,256]{1,0:T(8,128)(2,1)}), bf16[2048,256]{1,0:T(8,128)(2,1)}) %all-gather.13.cloned.1.call-update) | async-done | bytes 1048592 | tf_op jit(solution)/shard_map/all_gather | solution.py:72
  203.2 3.8 convolution_convert_fusion.1
  208.0 36.9 %all_gather.40 = bf16[512,768]{1,0:T(8,128)(2,1)S(1)} all-gather(bf16[16,768]{1,0:T(8,128)(2,1)S(1)} %pad_maximum_fusion.4), channel_id=1, replica_groups=mesh['seq'=32,'tensor'=8] {'seq'}, dimensions={0}, use_global_device_ids=true | all-gather | bytes 811008 | tf_op jit(solution)/shard_map/all_gather | solution.py:83
  255.8 36.7 %all-gather = f32[16384,2]{0,1:T(2,128)S(1)} all-gather(f32[512,2]{0,1:T(2,128)S(1)} %bitcast.125), channel_id=2, replica_groups=mesh['seq'=32,'tensor'=8] {'seq'}, dimensions={0}, use_global_device_ids=true | all-gather | bytes 135168 | tf_op jit(solution)/shard_map/all_gather | solution.py:37
  295.8 35.7 %all-gather.1 = f32[16384,2]{0,1:T(2,128)S(1)} all-gather(f32[512,2]{0,1:T(2,128)S(1)} %bitcast.128), channel_id=3, replica_groups=mesh['seq'=32,'tensor'=8] {'seq'}, dimensions={0}, use_global_device_ids=true | all-gather | bytes 135168 | tf_op jit(solution)/shard_map/all_gather | solution.py:37
  333.7 22.7 %while.33 = (s32[]{:T(128)}, bf16[2,512,256]{2,1,0:T(8,128)(2,1)}, s32[2]{0:T(128)}, bf16[1536,512]{1,0:T(8,128)(2,1)S(1)}, s32[]{:T(128)}, /*index=5*/bf16[1040...) while((s32[]{:T(128)}, bf16[2,512,256]{2,1,0:T(8,128)(2,1)}, ...), condition=%wide.region_4.5_spmd.clone, body=%wide.region_0.4_spmd.clone.sunk | while | flops 819334656 | bytes 41282024 | solution.py:145
  356.4 48.2 %all-gather.17.cloned.1.call-done = f32[16384,2,128]{0,2,1:T(8,128)} async-done(((f32[512,2,128]{0,2,1:T(8,128)}), f32[16384,2,128]{0,2,1:T(8,128)}) %all-gather.17.cloned.1.call-update) | async-done | bytes 16777232 | tf_op jit(solution)/shard_map/all_gather | solution.py:37
  406.0 25.0 %copy.46 = f32[16384,2,128]{2,1,0:T(2,128)} copy(f32[16384,2,128]{0,2,1:T(8,128)} %all-gather.17.cloned.1.call-done) | data formatting | bytes 33554432 | tf_op jit(solution)/shard_map/while | solution.py:42
  430.9 140.4 %while.32 = (s32[]{:T(128)}, f32[512,2]{0,1:T(2,128)S(1)}, f32[512,2]{0,1:T(2,128)S(1)}, f32[512,2,128]{2,1,0:T(2,128)S(1)}, f32[32,512,2]{1,2,0:T(2,128)S(1)}, ...) while((s32[]{:T(128)}, f32[512,2]{0,1:T(2,128)S(1)}, ...), condition=%wide.region_8.9_spmd, body=%wide.region_7.8_spmd.sunk | while | flops 399365 | bytes 1630351 | solution.py:42
  432.0 3.5 fusion.77
  436.5 3.5 fusion.77
  441.1 3.5 fusion.77
  445.6 3.5 fusion.77
  463.7 3.5 fusion.77
  468.2 3.5 fusion.77
  571.7 4.5 convolution_convert_fusion
  576.9 34.6 %reduce-scatter.2.cloned.1.call-done = bf16[1040,256]{1,0:T(8,128)(2,1)} async-done(((bf16[1040,2048]{1,0:T(8,128)(2,1)}), bf16[1040,256]{1,0:T(8,128)(2,1)}) %reduce-scatter.2.cloned.1.call-update) | async-done | bytes 532496 | tf_op jit(solution)/shard_map/reduce_scatter | solution.py:186
  612.8 15.4 %psum.7 = f32[1040]{0:T(1024)S(1)} all-reduce(f32[1040]{0:T(1024)S(1)} %multiply_reduce_fusion), channel_id=1, replica_groups=mesh['seq'=32,'tensor'=8] {'tensor'}, use_global_device_ids=true, to_apply=%region_11.12 | all-reduce | flops 1040 | bytes 8320 | tf_op jit(solution)/shard_map/psum | solution.py:190
  (257 shorter events, 172.2 us)
Async XLA Ops:
  7.2 45.1 %all-gather.9.cloned.1.call-start = ((), (), s32[]{:S(2)}) async-start(), calls=%async_computation.2 | async-start | bytes 4718592 | tf_op jit(solution)/shard_map/all_gather | solution.py:67
  7.9 118.8 %all-gather.11.cloned.1.call-start = ((), (), s32[]{:S(2)}) async-start(), calls=%async_computation.3 | async-start | bytes 1081344 | tf_op jit(solution)/shard_map/all_gather | solution.py:74
  10.5 120.1 %all-to-all-start = ((bf16[32,64,256]{2,1,0:T(8,128)(2,1)}), bf16[32,64,256]{2,1,0:T(8,128)(2,1)S(1)}, u32[]{:S(2)}, u32[]{:S(2)}) async-start(bf16[32,64,256]{2,1,0:T(8,128)(2,1)} %stack.2), calls=%async_computation | async-start | bytes 2097152 | tf_op jit(solution)/shard_map/all_to_all | solution.py:19
  22.5 180.7 %all-gather.13.cloned.1.call-start = ((), (), s32[]{:S(2)}) async-start(), calls=%async_computation.4 | async-start | bytes 1081344 | tf_op jit(solution)/shard_map/all_gather | solution.py:72
  23.3 381.4 %all-gather.17.cloned.1.call-start = ((), (), s32[]{:S(2)}) async-start(), calls=%async_computation.7 | async-start | bytes 17301504 | tf_op jit(solution)/shard_map/all_gather | solution.py:37
  24.0 33.0 %copy-start.11 = (f32[512]{0:T(512)}, f32[512]{0:T(512)S(1)}, u32[]{:S(2)}) copy-start(f32[512]{0:T(512)S(1)} %subtract_abs_fusion) | copy-start | bytes 6148
  38.3 18.7 %copy-start.14 = (f32[2]{0:T(128)}, f32[2]{0:T(128)S(1)}, u32[]{:S(2)}) copy-start(f32[2]{0:T(128)S(1)} %power_multiply_fusion) | copy-start | bytes 28
  38.3 207.4 %copy-start.13 = (f32[2,512]{1,0:T(2,128)}, f32[2,512]{1,0:T(2,128)S(1)}, u32[]{:S(2)}) copy-start(f32[2,512]{1,0:T(2,128)S(1)} %broadcast_multiply_fusion.1) | copy-start | bytes 12292
  208.0 39.7 %copy-start.8 = (bf16[1024,256]{0,1:T(8,128)(2,1)S(1)}, bf16[1024,256]{0,1:T(8,128)(2,1)}, u32[]{:S(2)}) copy-start(bf16[1024,256]{0,1:T(8,128)(2,1)} %copy.45) | copy-start | bytes 1572868
  245.8 2.0 copy-start
  249.8 321.9 %all-gather.15.cloned.1.call-start = ((), (), s32[]{:S(2)}) async-start(), calls=%async_computation.5 | async-start | bytes 1081344 | tf_op jit(solution)/shard_map/all_gather | solution.py:183
  250.4 361.1 %reduce-scatter.2.cloned.1.call-start = ((), (), s32[]{:S(2)}) async-start(), calls=%async_computation.6 | async-start | bytes 4792320 | tf_op jit(solution)/shard_map/reduce_scatter | solution.py:186
  250.5 81.0 %collective-permute-start = (bf16[256,512]{1,0:T(8,128)(2,1)S(1)}, bf16[256,512]{1,0:T(8,128)(2,1)S(1)}, u32[]{:S(2)}, u32[]{:S(2)}) collective-permute-start(bf16[256,512]{1,0:T(8,128)(2,1)S(1)} %get-tuple-element.403), channel_id=1, source_target_pairs={{0,8},{8,16},{16,24},{24,32},{32,40},{40,48},{48,56},{56,64},{64,7... | collective-permute-start | bytes 786440 | tf_op jit(solution)/shard_map/ppermute | solution.py:30
  252.9 79.2 %collective-permute-start.1 = (bf16[256,512]{1,0:T(8,128)(2,1)S(1)}, bf16[256,512]{1,0:T(8,128)(2,1)}, u32[]{:S(2)}, u32[]{:S(2)}) collective-permute-start(bf16[256,512]{1,0:T(8,128)(2,1)S(1)} %get-tuple-element.404), channel_id=1, source_target_pairs={{8,0},{16,8},{24,16},{32,24},{40,32},{48,40},{56,48},{64,56},{72,6... | collective-permute-start | bytes 786440 | tf_op jit(solution)/shard_map/ppermute | solution.py:31
  333.7 2.9 copy-start.3
  341.5 2.1 copy-start.9
  342.7 2.3 copy-start.4
  345.1 2.9 copy-start.3
  352.8 2.1 copy-start.9
  354.1 2.3 copy-start.4
  430.9 140.7 %copy-start.7 = (bf16[2,512,256]{2,1,0:T(8,128)(2,1)S(1)}, bf16[2,512,256]{2,1,0:T(8,128)(2,1)}, u32[]{:S(2)}) copy-start(bf16[2,512,256]{2,1,0:T(8,128)(2,1)} %get-tuple-element.294) | copy-start | bytes 1572868
  576.2 35.3 %copy-start.2 = (bf16[1024,256]{1,0:T(8,128)(2,1)S(1)}, bf16[1024,256]{1,0:T(8,128)(2,1)}, u32[]{:S(2)}) copy-start(bf16[1024,256]{1,0:T(8,128)(2,1)} %param.13) | copy-start | bytes 1572868
  576.2 35.3 %copy-start.12 = (bf16[16,256]{1,0:T(8,128)(2,1)S(1)}, bf16[16,256]{1,0:T(8,128)(2,1)}, u32[]{:S(2)}) copy-start(bf16[16,256]{1,0:T(8,128)(2,1)} %param.14) | copy-start | bytes 24580
  576.2 52.0 %copy-start.16 = (f32[256]{0:T(256)S(1)}, f32[256]{0:T(256)}, u32[]{:S(2)}) copy-start(f32[256]{0:T(256)} %param.19) | copy-start | bytes 3076
  (8 other events, 8.5 us)
Sparse Core Ops, SparseCore 0:
  9.8 42.4 all-gather.8
  54.8 71.8 all-gather.10
  129.3 73.8 all-gather.12
  249.9 154.7 all-gather.16
  407.1 68.5 all-gather.14
  576.4 35.1 reduce-scatter.1
